TPU v7x, 32 devices: a whole 2x2x4 slice. The times are simulated.
32 devices in a mesh: ctx: 8 (over y, x, core), fsdp: 4 (over z).
Axes of the slice: x: 2, y: 2, z: 4, core: 2. Of those that a mesh axis runs over, the one named last changes fastest.
Arguments:
- inner: bfloat16 [16384, 8192], P('ctx', 'fsdp'), may hold values from -6 to 6
- proj_weight: bfloat16 [32, 8192], P(None, 'fsdp'), may hold values from -0.0625 to 0.0625
- rates: float32 [8192], P('fsdp'), may hold values from 3.0517578e-06 to 0.0333333333
- keep: float32 [16384], P('ctx'), may hold values from 0.216 to 1, as said below
- skip: float32 [8192], P('fsdp'), may hold values from 0.5 to 1.5
- upstream: bfloat16 [16384, 8192], P('ctx', 'fsdp'), may hold values from -6 to 6
Outputs:
- input_grad: bfloat16 [16384, 8192], P('ctx', 'fsdp')
- proj_grad: float32 [32, 8192], P(None, 'fsdp')
Inputs may be any that keep to these rules, and one draw needn't show every extreme that they name: `keep`: factors on the tokens' decays.
All inputs are finite; a program needn't handle non-finite values.
Results may differ from a plain program's by a relative error of at most 0.0058.
Values sent between devices are 32-bit elements; how exact they have to be, the bound alone decides.
A program may use at most 128 MiB of HBM per device.

v0:
```python
import jax
import jax.numpy as jnp
from jax import lax
from jax.sharding import PartitionSpec as P

BLK = 256


def carried_in(shard, axis, combine, identity, reverse):
    length, place = (lax.axis_size(axis), lax.axis_index(axis))
    everything = jax.tree.map(lambda part: lax.all_gather(part, axis), shard)
    start = jax.tree.map(
        lambda part, zero: jnp.broadcast_to(jnp.asarray(zero, part.dtype), part.shape),
        shard,
        identity,
    )

    def step(k, before):
        at = length - 1 - k if reverse else k
        reached = at > place if reverse else at < place
        new = combine(before, jax.tree.map(lambda part: part[at], everything))
        return jax.tree.map(lambda a, b: jnp.where(reached, a, b), new, before)

    return lax.fori_loop(0, length, step, start)


def batched(form, left, right):
    return jnp.einsum(form, left, right, preferred_element_type=jnp.float32)


def precise(form, left, right):
    return jnp.einsum(
        form, left, right, precision=lax.Precision.HIGHEST, preferred_element_type=jnp.float32
    )


def combine(earlier, later):
    return (earlier[0] * later[0], later[1] + later[0][None, :] * earlier[1])


def local(inner, proj_weight, rates, keep, skip, upstream):
    length = inner.shape[0]
    channels = inner.shape[1]
    nstate = proj_weight.shape[0] // 2
    nblocks = length // BLK
    partial_coef = lax.dot_general(
        inner, proj_weight, (((1,), (1,)), ((), ())), preferred_element_type=jnp.float32
    )
    coeffs = lax.psum(partial_coef, "fsdp")
    coef_wide = coeffs.reshape(nblocks, BLK, 2 * nstate)
    write_wide = coef_wide[:, :, :nstate]
    read_wide = coef_wide[:, :, nstate:]
    coef_blocks = coeffs.astype(jnp.bfloat16).reshape(nblocks, BLK, 2 * nstate)
    write_coef = coef_blocks[:, :, :nstate]
    read_coef = coef_blocks[:, :, nstate:]
    factor = 1.0 / jnp.sqrt(jnp.float32(nstate))
    input_scale = jnp.sqrt(-jnp.expm1(-2.0 * rates))
    offsets = jnp.arange(1, BLK + 1).astype(jnp.float32)
    within_base = jnp.exp(-offsets[:, None] * rates[None, :])
    within = within_base[None] * jnp.cumprod(keep.reshape(nblocks, BLK), axis=1)[:, :, None]
    upstream_f = upstream.astype(jnp.float32).reshape(nblocks, BLK, channels)
    scaled = (
        input_scale[None, None, :]
        * inner.astype(jnp.float32).reshape(nblocks, BLK, channels)
        / within
    ).astype(jnp.bfloat16)
    weighted = (within * upstream_f).astype(jnp.bfloat16)
    decays = within[:, -1]
    state_terms = decays[:, None, :] * batched("jbn,jbe->jne", write_coef, scaled)
    adjoint_terms = factor * batched("jbn,jbe->jne", read_coef, weighted)

    def forward(state, item):
        return (item[0][None, :] * state + item[1], state)

    def backward(adjoint, item):
        return (item[1] + item[0][None, :] * adjoint, adjoint)

    zero_state = jnp.zeros((nstate, channels), jnp.float32)
    state_end, state_local = lax.scan(forward, zero_state, (decays, state_terms))
    adjoint_start, adjoint_local = lax.scan(
        backward, zero_state, (decays, adjoint_terms), reverse=True
    )
    device_decay = jnp.prod(decays, axis=0)
    ones_row = jnp.ones((1, channels), jnp.float32)
    before = jnp.concatenate([ones_row, jnp.cumprod(decays, axis=0)[:-1]], axis=0)
    after = jnp.flip(
        jnp.concatenate([ones_row, jnp.cumprod(jnp.flip(decays, 0), axis=0)[:-1]], axis=0), 0
    )
    identity = (jnp.ones_like(device_decay), zero_state)
    _, state_in = carried_in((device_decay, state_end), "ctx", combine, identity, False)
    _, adjoint_in = carried_in((device_decay, adjoint_start), "ctx", combine, identity, True)
    state_at = (state_local + before[:, None, :] * state_in[None]).astype(jnp.bfloat16)
    adjoint_at = adjoint_local + after[:, None, :] * adjoint_in[None]
    carried = (decays[:, None, :] * adjoint_at).astype(jnp.bfloat16)
    lower_mask = jnp.tril(jnp.ones((BLK, BLK), dtype=bool))
    read_write = jnp.where(
        lower_mask[None], batched("jbn,jcn->jbc", read_coef, write_coef), 0.0
    ).astype(jnp.bfloat16)
    grad_cross = jnp.where(lower_mask[None], batched("jbe,jce->jbc", weighted, scaled), 0.0)
    scan_grad = (
        input_scale[None, None, :]
        / within
        * (
            factor * batched("jbc,jbe->jce", read_write, weighted)
            + batched("jcn,jne->jce", write_coef, carried)
        )
    )
    grad_write = factor * precise("jbc,jbn->jcn", grad_cross, read_wide) + batched(
        "jce,jne->jcn", scaled, carried
    )
    grad_read = factor * (
        batched("jbe,jne->jbn", weighted, state_at)
        + precise("jbc,jcn->jbn", grad_cross, write_wide)
    )
    partial_grad = jnp.concatenate([grad_write, grad_read], axis=2).reshape(length, 2 * nstate)
    grad_coef = lax.psum(partial_grad, "fsdp")
    grad_short = grad_coef.astype(jnp.bfloat16)
    back_grad = jnp.dot(grad_short, proj_weight, preferred_element_type=jnp.float32)
    input_grad = (
        scan_grad.reshape(length, channels)
        + skip[None, :] * upstream_f.reshape(length, channels)
        + back_grad
    ).astype(jnp.bfloat16)
    local_proj = lax.dot_general(
        grad_coef,
        inner.astype(jnp.float32),
        (((0,), (0,)), ((), ())),
        precision=lax.Precision.HIGHEST,
        preferred_element_type=jnp.float32,
    )
    proj_total = lax.psum(local_proj, "ctx")
    return (input_grad, proj_total / (length * lax.axis_size("ctx")))


def solution(mesh):
    placed = (P("ctx", "fsdp"), P(None, "fsdp"), P("fsdp"), P("ctx"), P("fsdp"), P("ctx", "fsdp"))
    return jax.shard_map(
        local,
        mesh=mesh,
        in_specs=placed,
        out_specs=(P("ctx", "fsdp"), P(None, "fsdp")),
        check_vma=False,
    )
```

profile of v0, /device:TPU:0, one launch (start us, length us, event | category | flops | bytes accessed | tf_op | source)
XLA Modules:
  0.0 252.1 jit_solution(15752679022758044592)
XLA Ops:
  8.1 6.7 %fusion.49 = f32[2048,32]{0,1:T(8,128)} fusion(bf16[2048,2048]{1,0:T(8,128)(2,1)} %param.14, bf16[32,2048]{1,0:T(8,128)(2,1)S(1)} %copy-done), kind=kOutput, calls=%fused_computation.70 | convolution fusion | flops 268435456 | bytes 8781824 | tf_op jit(solution)/shard_map/dot_general | solution.py:46
  16.2 16.4 %fusion.4 = (bf16[8,256,2048]{2,1,0:T(8,128)(2,1)}, bf16[8,256,2048]{2,1,0:T(8,128)(2,1)S(1)}, f32[8,256,2048]{2,1,0:T(8,128)}) fusion(bf16[8,256,2048]{2,1,0:T(8,128)(2,1)} %bitcast.83, f32[8,256]{1,0:T(8,128)S(1)} %multiply_bitcast_fusion, f32[256,2048]{1,0:T(8,128)S(1)} %multiply_exponential_fusion, f32[2048]{0:T(1024)S(1)} %negate_sqrt_fusion, ...), kind=kLoop, calls=%fused_computation.17 | loop fusion | flops 33554432 | bytes 52445184 | tf_op jit(solution)/shard_map/convert_element_type | solution.py:66
  32.6 10.1 %fusion.50 = f32[8,256,256]{2,1,0:T(8,128)} fusion(bf16[8,256,2048]{2,1,0:T(8,128)(2,1)S(1)} %get-tuple-element.481, bf16[8,256,2048]{2,1,0:T(8,128)(2,1)} %get-tuple-element.480), kind=kOutput, calls=%fused_computation.71 | convolution fusion | flops 2147483648 | bytes 18874368 | tf_op jit(solution)/shard_map/jbe,jce->jbc/dot_general | solution.py:28
  42.7 1.1 slice_reduce_fusion.1
  44.2 10.7 %all-gather.1 = f32[16384]{0:T(1024)S(1)} all-gather(f32[2048]{0:T(1024)S(1)} %get-tuple-element.478), channel_id=3, replica_groups=mesh['ctx'=8,'fsdp'=4] {'ctx'}, dimensions={0}, use_global_device_ids=true | all-gather | bytes 73728 | tf_op jit(solution)/shard_map/all_gather | solution.py:11
  56.4 5.6 %convolution_multiply_fusion.1 = f32[8,16,2048]{2,1,0:T(8,128)} fusion(bf16[8,256,2048]{2,1,0:T(8,128)(2,1)} %copy-done.1, bf16[8,256,16]{1,0,2:T(8,128)(2,1)S(1)} %get-tuple-element.486), kind=kOutput, calls=%fused_computation.24 | convolution fusion | flops 134479872 | bytes 9502720 | tf_op jit(solution)/shard_map/jbn,jbe->jne/dot_general | solution.py:28
  62.0 8.3 %while.60 = (s32[]{:T(128)}, f32[16,2048]{1,0:T(8,128)S(1)}, f32[8,16,2048]{2,1,0:T(8,128)S(1)}, f32[8,16,2048]{2,1,0:T(8,128)}, f32[8,2048]{1,0:T(8,128)S(1)}, /*index=5*/s32[]{:T(128)}, s32[]{:T(128)}, s32[]{:T(128)}) while((s32[]{:T(128)}, f32[16,2048]{1,0:T(8,128)S(1)}, f32[8,16,2048]{2,1,0:T(8,128)S(1)}, ...), condition=%wide.region_4.5_spmd.clone, body=%wide.region_3.4_spmd.clone.sunk | while | flops 131076 | bytes 680056 | solution.py:80
  62.1 1.0 bitcast_add_fusion.7
  63.1 1.0 bitcast_add_fusion.7
  64.2 1.0 bitcast_add_fusion.7
  65.2 1.0 bitcast_add_fusion.7
  66.3 1.0 bitcast_add_fusion.7
  67.3 1.0 bitcast_add_fusion.7
  68.3 1.0 bitcast_add_fusion.7
  69.4 1.0 bitcast_add_fusion.7
  71.5 5.6 %convolution_multiply_fusion = f32[8,16,2048]{2,1,0:T(8,128)} fusion(bf16[8,256,2048]{2,1,0:T(8,128)(2,1)} %get-tuple-element.480, f32[8,2048]{1,0:T(8,128)S(1)} %get-tuple-element.713, bf16[8,256,16]{1,0,2:T(8,128)(2,1)S(1)} %get-tuple-element.485), kind=kOutput, calls=%fused_computation.23 | convolution fusion | flops 134479872 | bytes 9568256 | tf_op jit(solution)/shard_map/jbn,jbe->jne/dot_general | solution.py:28
  77.1 8.3 %while.62 = (s32[]{:T(128)}, f32[16,2048]{1,0:T(8,128)S(1)}, f32[8,16,2048]{2,1,0:T(8,128)S(1)}, f32[8,2048]{1,0:T(8,128)S(1)}, f32[8,16,2048]{2,1,0:T(8,128)}, /*index=5*/s32[]{:T(128)}, s32[]{:T(128)}) while((s32[]{:T(128)}, f32[16,2048]{1,0:T(8,128)S(1)}, f32[8,16,2048]{2,1,0:T(8,128)S(1)}, f32[8,2048]{1,0:T(8,128)S(1)}, ...), condition=%wide.region_10.11_spmd.clone, body=%wide.region_9.10_spmd.clone.sunk | while | flops 131075 | bytes 680036 | solution.py:79
  77.2 1.0 bitcast_add_fusion.8
  78.2 1.0 bitcast_add_fusion.8
  79.3 1.0 bitcast_add_fusion.8
  80.3 1.0 bitcast_add_fusion.8
  81.4 1.0 bitcast_add_fusion.8
  82.4 1.0 bitcast_add_fusion.8
  83.4 1.0 bitcast_add_fusion.8
  84.5 1.0 bitcast_add_fusion.8
  85.6 11.2 %fusion.11 = f32[8,256,2048]{2,1,0:T(8,128)} fusion(bf16[8,256,2048]{2,1,0:T(8,128)(2,1)} %copy-done.1, pred[256,256]{1,0:T(8,128)(4,1)S(1)} %iota_compare_fusion, bf16[8,256,16]{1,0,2:T(8,128)(2,1)S(1)} %get-tuple-element.486, bf16[8,256,16]{1,0,2:T(8,128)(2,1)S(1)} %get-tuple-element.485), kind=kOutput, calls=%fused_computation.31 | convolution fusion | flops 2165309440 | bytes 25362432 | tf_op jit(solution)/shard_map/jbc,jbe->jce/dot_general | solution.py:28
  96.9 8.2 %while.61 = (s32[]{:T(128)}, f32[16,2048]{1,0:T(8,128)S(1)}, s32[]{:T(128)}, f32[8,16,2048]{2,1,0:T(8,128)}, f32[8,2048]{1,0:T(8,128)S(1)}, /*index=5*/s32[]{:T(128)}, s32[]{:T(128)}, s32[]{:T(128)}, s32[]{:T(128)}) while((s32[]{:T(128)}, f32[16,2048]{1,0:T(8,128)S(1)}, s32[]{:T(128)}, f32[8,16,2048]{2,1,0:T(8,128)}, ...), condition=%wide.region_8.9_spmd.clone, body=%wide.region_7.8_spmd.clone.sunk | while | flops 131080 | bytes 417959 | solution.py:24
  96.9 1.0 fusion.66
  98.0 1.0 fusion.66
  99.0 1.0 fusion.66
  100.0 1.0 fusion.66
  101.1 1.0 fusion.66
  102.1 1.0 fusion.66
  103.1 1.0 fusion.66
  104.1 1.0 fusion.66
  105.1 15.6 %all-gather.8.cloned.1.call-done = f32[128,2048]{1,0:T(8,128)} async-done(((f32[16,2048]{1,0:T(8,128)}), f32[128,2048]{1,0:T(8,128)}) %all-gather.8.cloned.1.call-update) | async-done | bytes 1048592 | tf_op jit(solution)/shard_map/all_gather | solution.py:11
  120.7 8.1 %while.63 = (s32[]{:T(128)}, f32[16,2048]{1,0:T(8,128)S(1)}, s32[]{:T(128)}, f32[8,16,2048]{2,1,0:T(8,128)}, f32[8,2048]{1,0:T(8,128)S(1)}, /*index=5*/s32[]{:T(128)}, s32[]{:T(128)}) while((s32[]{:T(128)}, f32[16,2048]{1,0:T(8,128)S(1)}, s32[]{:T(128)}, f32[8,16,2048]{2,1,0:T(8,128)}, f32[8,2048]{1,0:T(8,128)S(1)}, ...), condition=%wide.region_13.14_spmd.clone, body=%wide.region_12.13_spmd.clone.sunk | while | flops 131076 | bytes 417897 | solution.py:24
  120.7 1.0 fusion.67
  128.8 5.9 %fusion.46 = f32[8,256,16]{1,2,0:T(8,128)S(1)} fusion(bf16[8,256,2048]{2,1,0:T(8,128)(2,1)} %get-tuple-element.480, f32[8,16,2048]{2,1,0:T(8,128)} %copy-done.8, f32[16,2048]{1,0:T(8,128)S(1)} %get-tuple-element.362, f32[8,2048]{1,0:T(8,128)S(1)} %rev.8, f32[8,2048]{1,0:T(8,128)S(1)} %get-tuple-element.714), kind=kOutput, calls=%fused_computation.67 | convolution fusion | flops 135266304 | bytes 9830400 | tf_op jit(solution)/shard_map/jce,jne->jcn/dot_general | solution.py:28
  134.7 3.1 %fusion.15 = f32[8,256,16]{1,2,0:T(8,128)S(1)} fusion(f32[8,256,16]{1,2,0:T(8,128)S(1)} %fusion.46, f32[8,256,256]{2,1,0:T(8,128)} %fusion.50, pred[256,256]{1,0:T(8,128)(4,1)S(1)} %iota_compare_fusion, f32[8,256,16]{1,0,2:T(8,128)S(1)} %get-tuple-element.483), kind=kOutput, calls=%fused_computation.33 | convolution fusion | flops 101253120 | bytes 2555904 | tf_op jit(solution)/shard_map/jbc,jbn->jcn/dot_general | solution.py:32
  137.8 5.9 %fusion.30 = f32[8,256,16]{1,2,0:T(8,128)S(1)} fusion(bf16[8,256,2048]{2,1,0:T(8,128)(2,1)} %copy-done.1, f32[8,16,2048]{2,1,0:T(8,128)} %copy-done.7, f32[16,2048]{1,0:T(8,128)S(1)} %get-tuple-element.365, f32[8,2048]{1,0:T(8,128)S(1)} %concatenate.10), kind=kOutput, calls=%fused_computation.44 | convolution fusion | flops 135004160 | bytes 9764864 | tf_op jit(solution)/shard_map/jbe,jne->jbn/dot_general | solution.py:28
  143.7 2.0 fusion.21
  146.8 12.0 %fusion.2 = f32[8,256,2048]{2,1,0:T(8,128)} fusion(f32[8,256,2048]{2,1,0:T(8,128)} %fusion.11, f32[8,256]{1,0:T(8,128)S(1)} %multiply_bitcast_fusion, f32[256,2048]{1,0:T(8,128)S(1)} %copy-done.5, f32[2048]{0:T(1024)S(1)} %negate_sqrt_fusion, bf16[8,256,16]{1,0,2:T(8,128)(2,1)S(1)} %get-tuple-element.485, f32[8,16,2048]{2,1,0:T(8,128)} %copy-done.8, ...), kind=kOutput, calls=%fused_computation.15 | convolution fusion | flops 156237824 | bytes 37044224 | tf_op jit(solution)/shard_map/jcn,jne->jce/dot_general | solution.py:28
  158.8 23.2 %all-reduce.8.cloned.1.call-done = f32[2048,32]{0,1:T(8,128)} async-done(((f32[2048,32]{0,1:T(8,128)}), f32[2048,32]{0,1:T(8,128)}) %all-reduce.8.cloned.1.call-update) | async-done | bytes 262160 | tf_op jit(solution)/shard_map/psum | solution.py:116
  182.0 8.4 %fusion.51 = f32[32,2048]{1,0:T(8,128)} fusion(f32[2048,32]{0,1:T(8,128)} %all-reduce.8.cloned.1.call-done, bf16[2048,2048]{1,0:T(8,128)(2,1)} %param.14), kind=kOutput, calls=%fused_computation.72 | convolution fusion | flops 1610612736 | bytes 8912896 | tf_op jit(solution)/shard_map/dot_general | solution.py:124
  190.5 13.2 %fusion.6 = bf16[2048,2048]{1,0:T(8,128)(2,1)} fusion(f32[8,256,2048]{2,1,0:T(8,128)} %fusion.2, bf16[32,2048]{1,0:T(8,128)(2,1)S(1)} %copy-done, f32[2048]{0:T(1024)S(1)} %copy-done.12, bf16[2048,2048]{1,0:T(8,128)(2,1)} %param.19, f32[2048,32]{0,1:T(8,128)S(1)} %copy-done.9), kind=kOutput, calls=%fused_computation.21 | convolution fusion | flops 289472512 | bytes 33955840 | tf_op jit(solution)/shard_map/dot_general | solution.py:118
  203.6 40.3 %all-reduce.10.cloned.1.call-done = f32[32,2048]{1,0:T(8,128)} async-done(((f32[32,2048]{1,0:T(8,128)}), f32[32,2048]{1,0:T(8,128)}) %all-reduce.10.cloned.1.call-update) | async-done | bytes 262160 | tf_op jit(solution)/shard_map/psum | solution.py:131
  243.9 1.7 broadcast_multiply_fusion.1
  (126 shorter events, 13.9 us)
Async XLA Ops:
  7.2 0.9 copy-start
  7.2 7.7 %copy-start.13 = (f32[2048]{0:T(1024)S(1)}, f32[2048]{0:T(1024)}, u32[]{:S(2)}) copy-start(f32[2048]{0:T(1024)} %param.17) | copy-start | bytes 24580
  7.2 8.6 %copy-start.11 = (f32[2048]{0:T(1024)S(1)}, f32[2048]{0:T(1024)}, u32[]{:S(2)}) copy-start(f32[2048]{0:T(1024)} %param.16) | copy-start | bytes 24580
  7.2 48.1 %all-reduce.6.cloned.1.call-start = ((), (), s32[]{:S(2)}) async-start(), calls=%async_computation | async-start | bytes 524288 | tf_op jit(solution)/shard_map/psum | solution.py:49
  14.8 82.1 %all-gather.6.cloned.1.call-start = ((), (), s32[]{:S(2)}) async-start(), calls=%async_computation.3 | async-start | bytes 1179648 | tf_op jit(solution)/shard_map/all_gather | solution.py:11
  16.1 16.4 %copy-start.4 = (f32[256,2048]{1,0:T(8,128)}, f32[256,2048]{1,0:T(8,128)S(1)}, u32[]{:S(2)}) copy-start(f32[256,2048]{1,0:T(8,128)S(1)} %multiply_exponential_fusion) | copy-start | bytes 6291460
  32.5 10.1 %copy-start.1 = (bf16[8,256,2048]{2,1,0:T(8,128)(2,1)}, bf16[8,256,2048]{2,1,0:T(8,128)(2,1)S(1)}, u32[]{:S(2)}) copy-start(bf16[8,256,2048]{2,1,0:T(8,128)(2,1)S(1)} %get-tuple-element.481) | copy-start | bytes 25165828
  70.4 0.7 copy-start.3
  70.4 1.1 copy-start.8
  71.0 14.4 %copy-start.10 = (f32[2048,32]{0,1:T(8,128)S(1)}, f32[2048,32]{0,1:T(8,128)}, u32[]{:S(2)}) copy-start(f32[2048,32]{0,1:T(8,128)} %all-reduce.6.cloned.1.call-done) | copy-start | bytes 786436
  71.1 49.7 %all-gather.8.cloned.1.call-start = ((), (), s32[]{:S(2)}) async-start(), calls=%async_computation.4 | async-start | bytes 1179648 | tf_op jit(solution)/shard_map/all_gather | solution.py:11
  85.5 11.3 %copy-start.2 = (f32[16,2048]{1,0:T(8,128)}, f32[16,2048]{1,0:T(8,128)S(1)}, u32[]{:S(2)}) copy-start(f32[16,2048]{1,0:T(8,128)S(1)} %get-tuple-element.364) | copy-start | bytes 393220
  85.5 11.3 %copy-start.7 = (f32[8,16,2048]{2,1,0:T(8,128)}, f32[8,16,2048]{2,1,0:T(8,128)S(1)}, u32[]{:S(2)}) copy-start(f32[8,16,2048]{2,1,0:T(8,128)S(1)} %get-tuple-element.363) | copy-start | bytes 3145732
  96.8 85.2 %all-reduce.8.cloned.1.call-start = ((), (), s32[]{:S(2)}) async-start(), calls=%async_computation.1 | async-start | bytes 524288 | tf_op jit(solution)/shard_map/psum | solution.py:116
  134.7 9.0 %copy-start.6 = (f32[8,256,256]{2,1,0:T(8,128)S(1)}, f32[8,256,256]{2,1,0:T(8,128)}, u32[]{:S(2)}) copy-start(f32[8,256,256]{2,1,0:T(8,128)} %fusion.50) | copy-start | bytes 6291460
  134.7 12.1 %copy-start.5 = (f32[256,2048]{1,0:T(8,128)S(1)}, f32[256,2048]{1,0:T(8,128)}, u32[]{:S(2)}) copy-start(f32[256,2048]{1,0:T(8,128)} %copy-done.4) | copy-start | bytes 6291460
  146.5 97.3 %all-reduce.10.cloned.1.call-start = ((), (), s32[]{:S(2)}) async-start(), calls=%async_computation.2 | async-start | bytes 524288 | tf_op jit(solution)/shard_map/psum | solution.py:131
  158.8 31.7 %copy-start.12 = (f32[2048]{0:T(1024)S(1)}, f32[2048]{0:T(1024)}, u32[]{:S(2)}) copy-start(f32[2048]{0:T(1024)} %param.18) | copy-start | bytes 24580
  182.0 8.5 %copy-start.9 = (f32[2048,32]{0,1:T(8,128)S(1)}, f32[2048,32]{0,1:T(8,128)}, u32[]{:S(2)}) copy-start(f32[2048,32]{0,1:T(8,128)} %all-reduce.8.cloned.1.call-done) | copy-start | bytes 786436
Sparse Core Ops, SparseCore 0:
  14.9 37.9 all-reduce.5
  71.2 23.7 all-gather.5
  97.0 23.6 all-gather.7
  146.7 35.2 all-reduce.7
  190.6 53.2 all-reduce.9
where the time goes:
time: 253 us; the launch traced here: 252 us
  matrix products  89.6 us (35%)
  waiting for transfers between devices  79.2 us (31%)
  other arithmetic  52.9 us (21%)
  between operations  14.1 us (6%)
  blocking collectives  10.7 us (4%)
  local copies, waits for them, and re-layouts  3.93 us (2%)
    dot_general x7, matrix products, batched(): return jnp.einsum(form, left, right, preferred_element_type=jnp.float32)  56.2 us
    psum x1, waiting for transfers between devices, local(): proj_total = lax.psum(local_proj, 'ctx')  40.3 us
    psum x1, waiting for transfers between devices, local(): grad_coef = lax.psum(partial_grad, 'fsdp')  23.2 us
    convert_element_type x1, other arithmetic, local(): scaled = (input_scale[None, None, :] * inner.astype(jnp.float32).reshape(...  16.4 us
    all_gather x2, waiting for transfers between devices, carried_in(): everything = jax.tree.map(lambda part: lax.all_gather(part, axis), shard)  15.6 us
    select_n x16, other arithmetic, step(): return jax.tree.map(lambda a, b: jnp.where(reached, a, b), new, before)  15.6 us
    dot_general x1, matrix products, local(): jnp.dot(grad_short, proj_weight, preferred_element_type=jnp.float32)  13.2 us
    all_gather x1, blocking collectives, carried_in(): everything = jax.tree.map(lambda part: lax.all_gather(part, axis), shard)  10.7 us
  transfers between devices with their start and end apart: 5, of which 3 were waited for; matrix products, arithmetic and copies ran while one was open for 35% of the time, Pallas kernels for 0%

commit v1 on v0

--- a/solution.py
+++ b/solution.py
@@ -128,7 +128,7 @@
         precision=lax.Precision.HIGHEST,
         preferred_element_type=jnp.float32,
     )
-    proj_total = lax.psum(local_proj, "ctx")
+    proj_total = jnp.sum(lax.all_gather(local_proj, "ctx"), axis=0)
     return (input_grad, proj_total / (length * lax.axis_size("ctx")))
 
 

time: 253 us -> 226 us (0.89)
  waiting for transfers between devices: 79.2 us -> 47.2 us
  other arithmetic: 52.9 us -> 58.8 us
    psum x1 -> x0, waiting for transfers between devices: 40.3 us -> none  [local(): proj_total = lax.psum(local_proj, 'ctx')]
    dynamic_update_slice x16, other arithmetic: 0.22 us -> 5.44 us  [local(): lax.scan(forward, zero_state, (decays, state_terms))]
    all_gather x2, waiting for transfers between devices: 15.6 us -> 20.2 us  [carried_in(): everything = jax.tree.map(lambda part: lax.all_gather(part, axis), shard)]
  transfers between devices with their start and end apart: 5 -> 5, of which waited for: 3 -> 4; matrix products, arithmetic and copies ran while one was open for 35% -> 42% of each run, Pallas kernels for 0% -> 0%
where the time goes in v1:
time: 226 us; the launch traced here: 225 us
  matrix products  87.2 us (39%)
  other arithmetic  58.8 us (26%)
  waiting for transfers between devices  47.2 us (21%)
  between operations  14.1 us (6%)
  blocking collectives  10.7 us (5%)
  local copies, waits for them, and re-layouts  5.25 us (2%)
    dot_general x7, matrix products, batched(): return jnp.einsum(form, left, right, preferred_element_type=jnp.float32)  55.5 us
    psum x1, waiting for transfers between devices, local(): grad_coef = lax.psum(partial_grad, 'fsdp')  24.5 us
    all_gather x2, waiting for transfers between devices, carried_in(): everything = jax.tree.map(lambda part: lax.all_gather(part, axis), shard)  20.2 us
    convert_element_type x1, other arithmetic, local(): scaled = (input_scale[None, None, :] * inner.astype(jnp.float32).reshape(...  16.4 us
    select_n x16, other arithmetic, step(): return jax.tree.map(lambda a, b: jnp.where(reached, a, b), new, before)  15.6 us
    dot_general x1, matrix products, local(): jnp.dot(grad_short, proj_weight, preferred_element_type=jnp.float32)  13.3 us
    all_gather x1, blocking collectives, carried_in(): everything = jax.tree.map(lambda part: lax.all_gather(part, axis), shard)  10.7 us
    dot_general x1, matrix products, local(): lax.dot_general(grad_coef, inner.astype(jnp.float32), (((0,), (0,)), ((),...  8.39 us
  transfers between devices with their start and end apart: 5, of which 4 were waited for; matrix products, arithmetic and copies ran while one was open for 42% of the time, Pallas kernels for 0%

profile of v1, /device:TPU:0, one launch (start us, length us, event | category | flops | bytes accessed | tf_op | source)
XLA Modules:
  0.0 225.0 jit_solution(17210717733900846874)
XLA Ops:
  8.1 6.7 %fusion.49 = f32[2048,32]{0,1:T(8,128)} fusion(bf16[2048,2048]{1,0:T(8,128)(2,1)} %param.14, bf16[32,2048]{1,0:T(8,128)(2,1)S(1)} %copy-done), kind=kOutput, calls=%fused_computation.70 | convolution fusion | flops 268435456 | bytes 8781824 | tf_op jit(solution)/shard_map/dot_general | solution.py:46
  16.2 16.4 %fusion.4 = (bf16[8,256,2048]{2,1,0:T(8,128)(2,1)}, bf16[8,256,2048]{2,1,0:T(8,128)(2,1)S(1)}, f32[8,256,2048]{2,1,0:T(8,128)}) fusion(bf16[8,256,2048]{2,1,0:T(8,128)(2,1)} %bitcast.84, f32[8,256]{1,0:T(8,128)S(1)} %multiply_bitcast_fusion, f32[256,2048]{1,0:T(8,128)S(1)} %multiply_exponential_fusion, f32[2048]{0:T(1024)S(1)} %negate_sqrt_fusion, ...), kind=kLoop, calls=%fused_computation.17 | loop fusion | flops 33554432 | bytes 52445184 | tf_op jit(solution)/shard_map/convert_element_type | solution.py:66
  32.6 10.1 %fusion.50 = f32[8,256,256]{2,1,0:T(8,128)} fusion(bf16[8,256,2048]{2,1,0:T(8,128)(2,1)S(1)} %get-tuple-element.481, bf16[8,256,2048]{2,1,0:T(8,128)(2,1)} %get-tuple-element.480), kind=kOutput, calls=%fused_computation.71 | convolution fusion | flops 2147483648 | bytes 18874368 | tf_op jit(solution)/shard_map/jbe,jce->jbc/dot_general | solution.py:28
  42.7 1.1 slice_reduce_fusion.1
  44.2 10.7 %all-gather.1 = f32[16384]{0:T(1024)S(1)} all-gather(f32[2048]{0:T(1024)S(1)} %get-tuple-element.478), channel_id=3, replica_groups=mesh['ctx'=8,'fsdp'=4] {'ctx'}, dimensions={0}, use_global_device_ids=true | all-gather | bytes 73728 | tf_op jit(solution)/shard_map/all_gather | solution.py:11
  56.4 5.6 %convolution_multiply_fusion.1 = f32[8,16,2048]{2,1,0:T(8,128)} fusion(bf16[8,256,2048]{2,1,0:T(8,128)(2,1)} %copy-done.1, bf16[8,256,16]{1,0,2:T(8,128)(2,1)S(1)} %get-tuple-element.486), kind=kOutput, calls=%fused_computation.24 | convolution fusion | flops 134479872 | bytes 9502720 | tf_op jit(solution)/shard_map/jbn,jbe->jne/dot_general | solution.py:28
  62.0 8.3 %while.60 = (s32[]{:T(128)}, f32[16,2048]{1,0:T(8,128)S(1)}, f32[8,16,2048]{2,1,0:T(8,128)S(1)}, f32[8,16,2048]{2,1,0:T(8,128)}, f32[8,2048]{1,0:T(8,128)S(1)}, /*index=5*/s32[]{:T(128)}, s32[]{:T(128)}, s32[]{:T(128)}) while((s32[]{:T(128)}, f32[16,2048]{1,0:T(8,128)S(1)}, f32[8,16,2048]{2,1,0:T(8,128)S(1)}, ...), condition=%wide.region_4.5_spmd.clone, body=%wide.region_3.4_spmd.clone.sunk | while | flops 131076 | bytes 680056 | solution.py:80
  62.1 1.0 bitcast_add_fusion.7
  63.1 1.0 bitcast_add_fusion.7
  64.2 1.0 bitcast_add_fusion.7
  65.2 1.0 bitcast_add_fusion.7
  66.3 1.0 bitcast_add_fusion.7
  67.3 1.0 bitcast_add_fusion.7
  68.3 1.0 bitcast_add_fusion.7
  69.4 1.0 bitcast_add_fusion.7
  71.1 5.7 %convolution_multiply_fusion = f32[8,16,2048]{2,1,0:T(8,128)} fusion(bf16[8,256,2048]{2,1,0:T(8,128)(2,1)} %get-tuple-element.480, f32[8,2048]{1,0:T(8,128)S(1)} %get-tuple-element.713, bf16[8,256,16]{1,0,2:T(8,128)(2,1)S(1)} %get-tuple-element.485), kind=kOutput, calls=%fused_computation.23 | convolution fusion | flops 134479872 | bytes 9568256 | tf_op jit(solution)/shard_map/jbn,jbe->jne/dot_general | solution.py:28
  76.8 1.1 broadcast.46.clone.1
  77.9 13.4 %while.62 = (s32[]{:T(128)}, f32[16,2048]{1,0:T(8,128)S(1)}, f32[8,16,2048]{2,1,0:T(8,128)}, f32[8,2048]{1,0:T(8,128)S(1)}, f32[8,16,2048]{2,1,0:T(8,128)}, /*index=5*/s32[]{:T(128)}, s32[]{:T(128)}) while((s32[]{:T(128)}, f32[16,2048]{1,0:T(8,128)S(1)}, f32[8,16,2048]{2,1,0:T(8,128)}, f32[8,2048]{1,0:T(8,128)S(1)}, ...), condition=%wide.region_10.11_spmd.clone, body=%wide.region_9.10_spmd.clone.sunk | while | flops 131075 | bytes 680544 | solution.py:79
  78.5 1.0 bitcast_add_fusion.8
  80.2 1.0 bitcast_add_fusion.8
  81.9 1.0 bitcast_add_fusion.8
  83.6 1.0 bitcast_add_fusion.8
  85.2 1.0 bitcast_add_fusion.8
  86.9 1.0 bitcast_add_fusion.8
  88.6 1.0 bitcast_add_fusion.8
  90.3 1.0 bitcast_add_fusion.8
  92.2 2.8 %all-gather.8.cloned.1.call-done = f32[128,2048]{1,0:T(8,128)} async-done(((f32[16,2048]{1,0:T(8,128)}), f32[128,2048]{1,0:T(8,128)}) %all-gather.8.cloned.1.call-update) | async-done | bytes 1048592 | tf_op jit(solution)/shard_map/all_gather | solution.py:11
  95.0 8.2 %while.61 = (s32[]{:T(128)}, f32[16,2048]{1,0:T(8,128)S(1)}, s32[]{:T(128)}, f32[8,16,2048]{2,1,0:T(8,128)}, f32[8,2048]{1,0:T(8,128)S(1)}, /*index=5*/s32[]{:T(128)}, s32[]{:T(128)}, s32[]{:T(128)}, s32[]{:T(128)}) while((s32[]{:T(128)}, f32[16,2048]{1,0:T(8,128)S(1)}, s32[]{:T(128)}, f32[8,16,2048]{2,1,0:T(8,128)}, ...), condition=%wide.region_8.9_spmd.clone, body=%wide.region_7.8_spmd.clone.sunk | while | flops 131080 | bytes 417959 | solution.py:24
  95.0 1.0 fusion.66
  96.0 1.0 fusion.66
  98.1 1.0 fusion.66
  99.1 1.0 fusion.66
  100.1 1.0 fusion.66
  101.2 1.0 fusion.66
  102.2 1.0 fusion.66
  103.2 17.4 %all-gather.10.cloned.1.call-done = f32[128,2048]{1,0:T(8,128)} async-done(((f32[16,2048]{1,0:T(8,128)}), f32[128,2048]{1,0:T(8,128)}) %all-gather.10.cloned.1.call-update) | async-done | bytes 1048592 | tf_op jit(solution)/shard_map/all_gather | solution.py:11
  120.6 8.1 %while.63 = (s32[]{:T(128)}, f32[16,2048]{1,0:T(8,128)S(1)}, s32[]{:T(128)}, f32[8,16,2048]{2,1,0:T(8,128)}, f32[8,2048]{1,0:T(8,128)S(1)}, /*index=5*/s32[]{:T(128)}, s32[]{:T(128)}) while((s32[]{:T(128)}, f32[16,2048]{1,0:T(8,128)S(1)}, s32[]{:T(128)}, f32[8,16,2048]{2,1,0:T(8,128)}, f32[8,2048]{1,0:T(8,128)S(1)}, ...), condition=%wide.region_13.14_spmd.clone, body=%wide.region_12.13_spmd.clone.sunk | while | flops 131076 | bytes 417897 | solution.py:24
  128.7 5.8 %fusion.46 = f32[8,256,16]{1,2,0:T(8,128)S(1)} fusion(bf16[8,256,2048]{2,1,0:T(8,128)(2,1)} %get-tuple-element.480, f32[8,16,2048]{2,1,0:T(8,128)S(1)} %get-tuple-element.360, f32[16,2048]{1,0:T(8,128)S(1)} %get-tuple-element.362, f32[8,2048]{1,0:T(8,128)S(1)} %rev.8, f32[8,2048]{1,0:T(8,128)S(1)} %get-tuple-element.714), kind=kOutput, calls=%fused_computation.67 | convolution fusion | flops 135266304 | bytes 9830400 | tf_op jit(solution)/shard_map/jce,jne->jcn/dot_general | solution.py:28
  134.5 5.7 %fusion.30 = f32[8,256,16]{1,2,0:T(8,128)S(1)} fusion(bf16[8,256,2048]{2,1,0:T(8,128)(2,1)} %copy-done.1, f32[8,16,2048]{2,1,0:T(8,128)S(1)} %copy-done.8, f32[16,2048]{1,0:T(8,128)S(1)} %get-tuple-element.365, f32[8,2048]{1,0:T(8,128)S(1)} %concatenate.10), kind=kOutput, calls=%fused_computation.44 | convolution fusion | flops 135004160 | bytes 9764864 | tf_op jit(solution)/shard_map/jbe,jne->jbn/dot_general | solution.py:28
  140.2 1.4 fusion.15
  141.6 2.0 fusion.21
  144.6 10.7 %fusion.11 = f32[8,256,2048]{2,1,0:T(8,128)} fusion(bf16[8,256,2048]{2,1,0:T(8,128)(2,1)} %copy-done.1, pred[256,256]{1,0:T(8,128)(4,1)S(1)} %iota_compare_fusion, bf16[8,256,16]{1,0,2:T(8,128)(2,1)S(1)} %get-tuple-element.486, bf16[8,256,16]{1,0,2:T(8,128)(2,1)S(1)} %get-tuple-element.485), kind=kOutput, calls=%fused_computation.31 | convolution fusion | flops 2165309440 | bytes 25362432 | tf_op jit(solution)/shard_map/jbc,jbe->jce/dot_general | solution.py:28
  155.3 24.5 %all-reduce.7.cloned.1.call-done = f32[2048,32]{0,1:T(8,128)} async-done(((f32[2048,32]{0,1:T(8,128)}), f32[2048,32]{0,1:T(8,128)}) %all-reduce.7.cloned.1.call-update) | async-done | bytes 262160 | tf_op jit(solution)/shard_map/psum | solution.py:116
  179.8 8.4 %fusion.51 = f32[32,2048]{1,0:T(8,128)} fusion(f32[2048,32]{0,1:T(8,128)} %all-reduce.7.cloned.1.call-done, bf16[2048,2048]{1,0:T(8,128)(2,1)} %param.14), kind=kOutput, calls=%fused_computation.72 | convolution fusion | flops 1610612736 | bytes 8912896 | tf_op jit(solution)/shard_map/dot_general | solution.py:124
  188.3 12.0 %fusion.2 = f32[8,256,2048]{2,1,0:T(8,128)} fusion(f32[8,256,2048]{2,1,0:T(8,128)} %fusion.11, f32[8,256]{1,0:T(8,128)S(1)} %multiply_bitcast_fusion, f32[256,2048]{1,0:T(8,128)S(1)} %copy-done.5, f32[2048]{0:T(1024)S(1)} %negate_sqrt_fusion, bf16[8,256,16]{1,0,2:T(8,128)(2,1)S(1)} %get-tuple-element.485, f32[8,16,2048]{2,1,0:T(8,128)} %copy-done.7, ...), kind=kOutput, calls=%fused_computation.15 | convolution fusion | flops 156237824 | bytes 37044224 | tf_op jit(solution)/shard_map/jcn,jne->jce/dot_general | solution.py:28
  200.2 13.3 %fusion.6 = bf16[2048,2048]{1,0:T(8,128)(2,1)} fusion(f32[8,256,2048]{2,1,0:T(8,128)} %fusion.2, bf16[32,2048]{1,0:T(8,128)(2,1)S(1)} %copy-done, f32[2048]{0:T(1024)S(1)} %copy-done.12, bf16[2048,2048]{1,0:T(8,128)(2,1)} %param.19, f32[2048,32]{0,1:T(8,128)S(1)} %copy-done.9), kind=kOutput, calls=%fused_computation.21 | convolution fusion | flops 289472512 | bytes 33955840 | tf_op jit(solution)/shard_map/dot_general | solution.py:118
  213.5 2.5 %all-gather.12.cloned.1.call-done = f32[256,2048]{1,0:T(8,128)} async-done(((f32[32,2048]{1,0:T(8,128)}), f32[256,2048]{1,0:T(8,128)}) %all-gather.12.cloned.1.call-update) | async-done | bytes 2097168 | tf_op jit(solution)/shard_map/all_gather | solution.py:131
  216.0 1.7 reduce_sum.9
  (127 shorter events, 22.0 us)
Async XLA Ops:
  7.2 0.9 copy-start
  7.2 7.7 %copy-start.13 = (f32[2048]{0:T(1024)S(1)}, f32[2048]{0:T(1024)}, u32[]{:S(2)}) copy-start(f32[2048]{0:T(1024)} %param.17) | copy-start | bytes 24580
  7.2 8.6 %copy-start.11 = (f32[2048]{0:T(1024)S(1)}, f32[2048]{0:T(1024)}, u32[]{:S(2)}) copy-start(f32[2048]{0:T(1024)} %param.16) | copy-start | bytes 24580
  7.2 48.1 %all-reduce.5.cloned.1.call-start = ((), (), s32[]{:S(2)}) async-start(), calls=%async_computation | async-start | bytes 524288 | tf_op jit(solution)/shard_map/psum | solution.py:49
  14.8 80.2 %all-gather.8.cloned.1.call-start = ((), (), s32[]{:S(2)}) async-start(), calls=%async_computation.2 | async-start | bytes 1179648 | tf_op jit(solution)/shard_map/all_gather | solution.py:11
  16.1 16.4 %copy-start.4 = (f32[256,2048]{1,0:T(8,128)}, f32[256,2048]{1,0:T(8,128)S(1)}, u32[]{:S(2)}) copy-start(f32[256,2048]{1,0:T(8,128)S(1)} %multiply_exponential_fusion) | copy-start | bytes 6291460
  32.5 10.1 %copy-start.1 = (bf16[8,256,2048]{2,1,0:T(8,128)(2,1)}, bf16[8,256,2048]{2,1,0:T(8,128)(2,1)S(1)}, u32[]{:S(2)}) copy-start(bf16[8,256,2048]{2,1,0:T(8,128)(2,1)S(1)} %get-tuple-element.481) | copy-start | bytes 25165828
  70.4 0.7 copy-start.3
  70.4 58.3 %copy-start.7 = (f32[8,16,2048]{2,1,0:T(8,128)}, f32[8,16,2048]{2,1,0:T(8,128)S(1)}, u32[]{:S(2)}) copy-start(f32[8,16,2048]{2,1,0:T(8,128)S(1)} %get-tuple-element.360) | copy-start | bytes 3145732
  71.0 20.2 %copy-start.10 = (f32[2048,32]{0,1:T(8,128)S(1)}, f32[2048,32]{0,1:T(8,128)}, u32[]{:S(2)}) copy-start(f32[2048,32]{0,1:T(8,128)} %all-reduce.5.cloned.1.call-done) | copy-start | bytes 786436
  71.1 49.5 %all-gather.10.cloned.1.call-start = ((), (), s32[]{:S(2)}) async-start(), calls=%async_computation.3 | async-start | bytes 1179648 | tf_op jit(solution)/shard_map/all_gather | solution.py:11
  91.3 0.7 copy-start.2
  91.9 42.6 %copy-start.8 = (f32[8,16,2048]{2,1,0:T(8,128)S(1)}, f32[8,16,2048]{2,1,0:T(8,128)}, u32[]{:S(2)}) copy-start(f32[8,16,2048]{2,1,0:T(8,128)} %get-tuple-element.363) | copy-start | bytes 3145732
  91.9 87.9 %all-reduce.7.cloned.1.call-start = ((), (), s32[]{:S(2)}) async-start(), calls=%async_computation.1 | async-start | bytes 524288 | tf_op jit(solution)/shard_map/psum | solution.py:116
  128.7 11.5 %copy-start.6 = (f32[8,256,256]{2,1,0:T(8,128)S(1)}, f32[8,256,256]{2,1,0:T(8,128)}, u32[]{:S(2)}) copy-start(f32[8,256,256]{2,1,0:T(8,128)} %fusion.50) | copy-start | bytes 6291460
  144.3 71.7 %all-gather.12.cloned.1.call-start = ((), (), s32[]{:S(2)}) async-start(), calls=%async_computation.4 | async-start | bytes 2359296 | tf_op jit(solution)/shard_map/all_gather | solution.py:131
  155.3 32.9 %copy-start.5 = (f32[256,2048]{1,0:T(8,128)S(1)}, f32[256,2048]{1,0:T(8,128)}, u32[]{:S(2)}) copy-start(f32[256,2048]{1,0:T(8,128)} %copy-done.4) | copy-start | bytes 6291460
  188.2 12.0 %copy-start.9 = (f32[2048,32]{0,1:T(8,128)S(1)}, f32[2048,32]{0,1:T(8,128)}, u32[]{:S(2)}) copy-start(f32[2048,32]{0,1:T(8,128)} %all-reduce.7.cloned.1.call-done) | copy-start | bytes 786436
  188.2 12.0 %copy-start.12 = (f32[2048]{0:T(1024)S(1)}, f32[2048]{0:T(1024)}, u32[]{:S(2)}) copy-start(f32[2048]{0:T(1024)} %param.18) | copy-start | bytes 24580
Sparse Core Ops, SparseCore 0:
  14.9 37.9 all-reduce.4
  71.2 23.7 all-gather.7
  97.0 23.4 all-gather.9
  144.5 35.2 all-reduce.6
  188.3 27.6 all-gather.11
